TPU v7x, 512 devices: a whole 4x4x16 slice. The times are simulated.
512 devices in a mesh: query: 32 (over z, core), passage: 16 (over x, y).
Axes of the slice: x: 4, y: 4, z: 16, core: 2. Of those that a mesh axis runs over, the one named last changes fastest.
Arguments:
- queries: bfloat16 [2048, 32, 128], P(('query', 'passage')), may hold values from -60 to 60
- hidden: bfloat16 [2048, 180, 768], P(('query', 'passage')), may hold values from -24 to 24
- proj: bfloat16 [768, 128], replicated, may hold values from -0.21875 to 0.21875
- lists: int32 [2048, 64], P(('query', 'passage')), may hold values from 0 to 63
Outputs:
- losses: float32 [2048], P(('query', 'passage'))
- w_grad: float32 [768, 128], P('passage')
Inputs may be any that keep to these rules, and one draw needn't show every extreme that they name: `lists`: queries of one row only list passages of that same row; entry 0 of each list is the query's positive passage.
All inputs are finite; a program needn't handle non-finite values.
Results may differ from a plain program's by a relative error of at most 0.0075.
The roundings to bfloat16 on the way count: a program that leaves them out, or rounds other values in their place, can miss the bound.
Values may be sent and summed in bfloat16 or wider, within the bound.
A program may use at most 64 MiB of HBM per device.

v0:
```python
import jax
import jax.numpy as jnp
from jax import lax
from jax.sharding import PartitionSpec as P

BETA = 4.0
EPS = 1e-06


def body(queries, hidden, proj, lists):
    qcount, qtok, width = queries.shape
    pcount, ptok, hwidth = hidden.shape
    nside = lax.axis_size("passage")
    prow = pcount * nside
    total = qcount * lax.axis_size("query") * nside
    hidden_flat = hidden.reshape(-1, hwidth)
    flat = jnp.dot(hidden_flat, proj, preferred_element_type=jnp.float32)
    norm = jnp.sqrt(jnp.sum(flat * flat, axis=1, keepdims=True) + EPS)
    unit = flat / norm
    embed = unit.astype(jnp.bfloat16).reshape(pcount, ptok, width)
    gathered = lax.all_gather(queries, "passage", axis=0, tiled=True)
    qflat = gathered.reshape(-1, width)

    def score_single(emb):
        sims = lax.dot_general(
            emb, qflat, (((1,), (1,)), ((), ())), preferred_element_type=jnp.float32
        )
        lse = jax.nn.logsumexp(BETA * sims, axis=0)
        return jnp.sum(lse.reshape(-1, qtok), axis=1) / BETA

    scores = lax.map(score_single, embed).T
    mine = lax.all_to_all(scores, "passage", split_axis=0, concat_axis=1, tiled=True)
    columns = jnp.arange(prow, dtype=jnp.int32)
    onehot = (lists[:, :, None] == columns[None, None, :]).astype(jnp.float32)
    listed = jnp.einsum("qkp,qp->qk", onehot, mine, precision=lax.Precision.HIGHEST)
    losses = jax.nn.logsumexp(listed, axis=1) - listed[:, 0]
    probs = jax.nn.softmax(listed, axis=1)
    target = (jnp.arange(listed.shape[1], dtype=jnp.int32) == 0).astype(jnp.float32)
    coef = (
        jnp.einsum("qkp,qk->qp", onehot, probs - target[None, :], precision=lax.Precision.HIGHEST)
        / total
    )
    coef_home = lax.all_to_all(coef, "passage", split_axis=1, concat_axis=0, tiled=True)
    grad_qflat = gathered.reshape(-1, width)

    def grad_single(args):
        emb, column = args
        sims = lax.dot_general(
            emb, grad_qflat, (((1,), (1,)), ((), ())), preferred_element_type=jnp.float32
        )
        probs = jax.nn.softmax(BETA * sims, axis=0)
        weight = (probs * jnp.repeat(column, qtok)[None, :]).astype(jnp.bfloat16)
        return jnp.dot(weight, grad_qflat, preferred_element_type=jnp.float32)

    d_embed = lax.map(grad_single, (embed, coef_home.T))
    d_rows = d_embed.reshape(-1, width)
    d_flat = ((d_rows - unit * jnp.sum(d_rows * unit, axis=1, keepdims=True)) / norm).astype(
        jnp.bfloat16
    )
    partial_grad = lax.dot_general(
        hidden_flat, d_flat, (((0,), (0,)), ((), ())), preferred_element_type=jnp.float32
    )
    share = hwidth // nside
    full_grad = lax.psum(partial_grad, ("query", "passage"))
    w_grad = lax.dynamic_slice_in_dim(full_grad, lax.axis_index("passage") * share, share, 0)
    return (losses, w_grad)


def solution(mesh):
    placed = (
        P(("query", "passage"), None, None),
        P(("query", "passage"), None, None),
        P(),
        P(("query", "passage"), None),
    )
    return jax.shard_map(
        body,
        mesh=mesh,
        in_specs=placed,
        out_specs=(P(("query", "passage")), P("passage", None)),
        check_vma=False,
    )
```

profile of v0, /device:TPU:1, one launch (start us, length us, event | category | flops | bytes accessed | tf_op | source)
XLA Modules:
  0.0 560.6 jit_solution(6270691283780664740)
XLA Ops:
  7.2 1.4 copy.11
  10.2 20.0 %all_gather.3 = bf16[64,32,128]{2,1,0:T(8,128)(2,1)S(1)} all-gather(bf16[4,32,128]{2,1,0:T(8,128)(2,1)S(1)} %copy-done.6), channel_id=1, replica_groups=mesh['query'=32,'passage'=16] {'passage'}, dimensions={0}, use_global_device_ids=true | all-gather | bytes 557056 | tf_op jit(solution)/shard_map/all_gather | solution.py:21
  30.2 4.4 while.20
  35.3 4.9 all-to-all-start
  40.2 6.5 %all-to-all-done = f32[16,4,4]{1,2,0:T(4,128)S(1)} async-done(((f32[16,4,4]{1,2,0:T(4,128)}), f32[16,4,4]{1,2,0:T(4,128)S(1)}, u32[]{:S(2)}, u32[]{:S(2)}) %all-to-all-start) | async-done | bytes 1056 | tf_op jit(solution)/shard_map/all_to_all | solution.py:32
  47.2 0.6 fusion.17
  49.0 3.5 all-to-all-start.1
  52.5 6.3 %all-to-all-done.1 = f32[4,16,4]{2,0,1:T(4,128)S(1)} async-done(((f32[4,16,4]{2,0,1:T(4,128)}), f32[4,16,4]{2,0,1:T(4,128)S(1)}, u32[]{:S(2)}, u32[]{:S(2)}) %all-to-all-start.1) | async-done | bytes 1056 | tf_op jit(solution)/shard_map/all_to_all | solution.py:43
  59.0 16.0 %while.21 = (s32[]{:T(128)}, f32[4,180,128]{2,1,0:T(8,128)}, bf16[4,180,128]{2,1,0:T(8,128)(2,1)S(1)}, bf16[2048,128]{1,0:T(8,128)(2,1)S(1)}, f32[4,64]{1,0:T(4,128)S(1)}, /*index=5*/s32[]{:T(128)}) while((s32[]{:T(128)}, f32[4,180,128]{2,1,0:T(8,128)}, bf16[4,180,128]{2,1,0:T(8,128)(2,1)S(1)}, bf16[2048,128]{1,0:T(8,128)(2,1)S(1)}, ...), condition=%wide.region_12.13_spmd, body=%wide.region_9.0_spmd.sunk | while | flops 191688704 | bytes 5761993 | solution.py:55
  59.0 1.1 fusion.44
  60.2 0.7 mul.57
  60.8 1.0 fusion.46
  61.9 1.1 fusion.47
  63.0 1.1 fusion.44
  64.2 0.7 mul.57
  64.8 1.0 fusion.46
  65.9 1.1 fusion.47
  67.0 1.1 fusion.44
  68.2 0.7 mul.57
  68.9 1.0 fusion.46
  69.9 1.1 fusion.47
  71.0 1.1 fusion.44
  72.2 0.7 mul.57
  72.9 1.0 fusion.46
  73.9 1.1 fusion.47
  75.0 1.0 reshape.67
  76.0 1.3 multiply_reduce_fusion
  77.3 2.3 convolution_bitcast_fusion.1
  79.7 1.2 fusion.18
  80.9 471.2 %all-reduce.2.cloned.1.call-done = f32[768,128]{0,1:T(8,128)} async-done(((f32[768,128]{0,1:T(8,128)}), f32[768,128]{0,1:T(8,128)}) %all-reduce.2.cloned.1.call-update) | async-done | bytes 393232 | tf_op jit(solution)/shard_map/psum | solution.py:64
  552.0 1.0 constant_dynamic-slice_fusion.1
  553.0 0.7 copy.16
  (118 shorter events, 8.6 us)
Async XLA Ops:
  7.2 1.7 copy-start
  8.9 1.3 copy-start.6
  9.4 0.7 copy-start.1
  9.5 0.7 copy-start.5
  30.2 16.6 %copy-start.12 = (s32[4,64]{1,0:T(4,128)S(1)}, s32[4,64]{1,0:T(4,128)}, u32[]{:S(2)}) copy-start(s32[4,64]{1,0:T(4,128)} %param.11) | copy-start | bytes 3076
  35.3 11.4 %all-to-all-start = ((f32[16,4,4]{1,2,0:T(4,128)}), f32[16,4,4]{1,2,0:T(4,128)S(1)}, u32[]{:S(2)}, u32[]{:S(2)}) async-start(f32[16,4,4]{1,2,0:T(4,128)} %copy.12), calls=%async_computation | async-start | bytes 65536 | tf_op jit(solution)/shard_map/all_to_all | solution.py:32
  47.1 11.8 %copy-start.3 = (f32[4,1,64]{0,2,1:T(8,128)}, f32[4,1,64]{0,2,1:T(8,128)S(1)}, u32[]{:S(2)}) copy-start(f32[4,1,64]{0,2,1:T(8,128)S(1)} %copy.18) | copy-start | bytes 3076
  47.2 0.6 copy-start.7
  49.0 9.9 %all-to-all-start.1 = ((f32[4,16,4]{2,0,1:T(4,128)}), f32[4,16,4]{2,0,1:T(4,128)S(1)}, u32[]{:S(2)}, u32[]{:S(2)}) async-start(f32[4,16,4]{2,0,1:T(4,128)} %copy.14), calls=%async_computation.1 | async-start | bytes 65536 | tf_op jit(solution)/shard_map/all_to_all | solution.py:43
  52.5 499.6 %all-reduce.2.cloned.1.call-start = ((), (), s32[]{:S(2)}) async-start(), calls=%async_computation.2 | async-start | bytes 786432 | tf_op jit(solution)/shard_map/psum | solution.py:64
  59.0 1.1 copy-start.10
  60.8 1.0 copy-start.2
  60.8 1.0 copy-start.4
  61.9 1.1 copy-start.11
  63.0 1.1 copy-start.10
  64.8 1.0 copy-start.2
  64.8 1.0 copy-start.4
  65.9 1.1 copy-start.11
  67.0 1.1 copy-start.10
  68.9 1.0 copy-start.2
  68.9 1.0 copy-start.4
  69.9 1.1 copy-start.11
  71.0 1.1 copy-start.10
  72.9 1.0 copy-start.2
  72.9 1.0 copy-start.4
  73.9 1.1 copy-start.11
  77.3 2.4 copy-start.8
  77.3 2.4 copy-start.9
Sparse Core Ops, SparseCore 0:
  79.8 472.2 all-reduce.1
where the time goes:
time: 562 us; the launch traced here: 561 us
  waiting for transfers between devices  484 us (86%)
  blocking collectives  20 us (4%)
  matrix products  14.4 us (3%)
  between operations  14.2 us (3%)
  local copies, waits for them, and re-layouts  10.5 us (2%)
  other arithmetic  8.8 us (2%)
  starting transfers between devices  8.45 us (2%)
    psum x1, waiting for transfers between devices, body(): full_grad = lax.psum(partial_grad, ('query', 'passage'))  471 us
    all_gather x1, blocking collectives, body(): gathered = lax.all_gather(queries, 'passage', axis=0, tiled=True)  20 us
  transfers between devices with their start and end apart: 3, of which 3 were waited for; matrix products, arithmetic and copies ran while one was open for 0% of the time, Pallas kernels for 0%

commit v1 on v0

v1 whole, which is shorter than its diff:
```python
import functools

import jax
import jax.numpy as jnp
from jax import lax
from jax.experimental import pallas as pl
from jax.experimental.pallas import tpu as pltpu
from jax.sharding import PartitionSpec as P

BETA = 4.0
EPS = 1e-06
SIDE = 4
ROWS = SIDE * SIDE
F32 = jnp.float32
BF16 = jnp.bfloat16
NEGBIG = -3.0e38
MESH = pl.DeviceIdType.MESH


def gray(index):
    return index ^ (index >> 1)


def spread(tile, lane, block):
    own = jnp.where(lane // 8 == block, tile, 0.0)
    for step in (8, 16, 32, 64):
        own = own + pltpu.roll(own, step, 1)
    return own


def kernel(
    total,
    queries_ref, hidden_ref, proj_ref, lists_ref,
    loss_ref, grad_ref,
    qbuf, meta, mrows, mcols, embed, unit, norm, expo, rsum, score, scale,
    part, precv, rsend, rrecv, zbuf, fin,
    qs, qr, ms, mr, ss, sr, ps, rs, rr, zs, zr, fs,
):
    qcount, qtok, width = queries_ref.shape
    pcount, ptok, hwidth = hidden_ref.shape
    nz = lax.axis_size("query") // 2
    qid = lax.axis_index("query")
    me = lax.axis_index("passage")
    mx, my = me // SIDE, me % SIDE
    mz, core = qid // 2, qid % 2
    partner = {"query": mz * 2 + (1 - core)}
    block = qcount * qtok
    half = grad_ref.shape[0] // 2

    def peer_of(slot):
        dx, dy = gray(slot // SIDE), gray(slot % SIDE)
        return ((mx + dx) % SIDE) * SIDE + (my + dy) % SIDE

    def back_of(slot):
        dx, dy = gray(slot // SIDE), gray(slot % SIDE)
        return ((mx + SIDE - dx) % SIDE) * SIDE + (my + SIDE - dy) % SIDE

    barrier = pltpu.get_barrier_semaphore()
    for slot in range(1, ROWS):
        pl.semaphore_signal(barrier, inc=1, device_id={"passage": peer_of(slot)}, device_id_type=MESH)

    def greet(step, carry):
        zpeer = (mz + step) % nz
        pl.semaphore_signal(barrier, inc=1, device_id={"query": zpeer * 2 + core}, device_id_type=MESH)
        return carry

    lax.fori_loop(1, nz, greet, 0)
    pl.semaphore_signal(barrier, inc=1, device_id=partner, device_id_type=MESH)

    lane = lax.broadcasted_iota(jnp.int32, (8, 128), 1)
    row = lax.broadcasted_iota(jnp.int32, (block, block), 0)
    col = lax.broadcasted_iota(jnp.int32, (block, block), 1)
    order = jnp.where(col == (row % qcount) * qtok + row // qcount, 1.0, 0.0).astype(BF16)
    mine = jnp.dot(order, queries_ref[...].reshape(block, width), preferred_element_type=F32)
    qbuf[0:block, :] = mine.astype(BF16)

    listed = jnp.concatenate(
        [lists_ref[...].astype(F32), jnp.zeros((qcount, 128 - lists_ref.shape[1]), F32)], axis=1
    )
    listed = jnp.concatenate([listed, jnp.zeros((128 - qcount, 128), F32)], axis=0).T
    listed = listed[: lists_ref.shape[1], :]
    lrow = lax.broadcasted_iota(jnp.int32, (lists_ref.shape[1], 128), 1)
    number = jnp.where(lrow % 8 < pcount, (lrow // 8) * pcount + lrow % 8, -1).astype(F32)
    counts, firsts = [], []
    for query in range(qcount):
        hit = jnp.where(listed[:, query : query + 1] == number, 1.0, 0.0)
        counts.append(jnp.sum(hit, axis=0, keepdims=True))
        firsts.append(hit[0:1, :])
    tile = jnp.concatenate(counts + firsts, axis=0)
    meta[0] = jnp.concatenate([tile, jnp.zeros_like(tile)], axis=0).astype(BF16)

    pl.semaphore_wait(barrier, ROWS - 1 + nz - 1 + 1)

    def query_copy(slot):
        return pltpu.make_async_remote_copy(
            src_ref=qbuf.at[pl.ds(0, block)],
            dst_ref=qbuf.at[pl.ds(slot * block, block)],
            send_sem=qs.at[slot], recv_sem=qr.at[slot],
            device_id={"passage": back_of(slot)}, device_id_type=MESH,
        )

    def meta_copy(slot):
        return pltpu.make_async_remote_copy(
            src_ref=meta.at[0], dst_ref=meta.at[slot],
            send_sem=ms.at[slot], recv_sem=mr.at[slot],
            device_id={"passage": back_of(slot)}, device_id_type=MESH,
        )

    def score_copy(slot):
        return pltpu.make_async_remote_copy(
            src_ref=score.at[0], dst_ref=score.at[slot],
            send_sem=ss.at[slot], recv_sem=sr.at[slot],
            device_id={"passage": back_of(slot)}, device_id_type=MESH,
        )

    for slot in range(1, ROWS):
        query_copy(slot).start()
    for slot in range(1, ROWS):
        meta_copy(slot).start()

    def project(passage, carry):
        flat = jnp.dot(hidden_ref[passage], proj_ref[...], preferred_element_type=F32)
        size = jnp.sqrt(jnp.sum(flat * flat, axis=1, keepdims=True) + EPS)
        one = flat / size
        norm[passage] = jnp.broadcast_to(size, one.shape)
        unit[passage] = one
        embed[passage] = one.astype(BF16)
        return carry

    lax.fori_loop(0, pcount, project, 0)

    def score_pair(pair, found):
        @pl.when(pair > 0)
        def _():
            query_copy(2 * pair).wait_recv()

        query_copy(2 * pair + 1).wait_recv()
        start = pl.multiple_of(pair * 2 * block, 2 * block)
        both = qbuf[pl.ds(start, 2 * block), :]
        lses = []
        for passage in range(pcount):
            sims = lax.dot_general(
                embed[passage], both, (((1,), (1,)), ((), ())), preferred_element_type=F32
            )
            top = jnp.max(sims, axis=0, keepdims=True)
            raised = jnp.exp(BETA * (sims - top))
            expo[pair, passage] = raised
            total_e = jnp.sum(raised, axis=0, keepdims=True)
            rsum[pair, passage : passage + 1] = 1.0 / total_e
            lses.append(jnp.log(total_e) + BETA * top)
        lse = jnp.concatenate(lses + lses, axis=0)
        for which in range(2):
            summed = lse[:, which * block : (which + 1) * block]
            for step in (4, 8, 16, 32, 64):
                summed = summed + pltpu.roll(summed, step, 1)
            found = jnp.where(lane // 8 == peer_of(2 * pair + which), summed, found)
        return found

    found = lax.fori_loop(0, ROWS // 2, score_pair, jnp.zeros((8, 128), F32))
    score[0] = found / BETA

    for slot in range(1, ROWS):
        score_copy(slot).start()

    for slot in range(ROWS):
        if slot:
            meta_copy(slot).wait_recv()
        mrows[pl.ds(pl.multiple_of(8 * peer_of(slot), 8), 8), :] = meta[slot].astype(F32)[0:8]
    mcols[...] = mrows[...].T

    top = jnp.full((8, 128), NEGBIG, F32)
    for slot in range(ROWS):
        if slot:
            score_copy(slot).wait_recv()
        count = mcols[pl.ds(pl.multiple_of(8 * peer_of(slot), 8), 8), :]
        top = jnp.maximum(top, jnp.where(count > 0, score[slot], NEGBIG))
    top = jnp.max(top, axis=0, keepdims=True)
    mass = jnp.zeros((8, 128), F32)
    shares = None
    for slot in range(ROWS):
        count = mcols[pl.ds(pl.multiple_of(8 * peer_of(slot), 8), 8), :]
        term = jnp.where(count > 0, count * jnp.exp(jnp.where(count > 0, score[slot], top) - top), 0.0)
        mass = mass + term
        if slot == 0:
            shares = term
    mass = jnp.sum(mass, axis=0, keepdims=True)
    top, mass = jnp.broadcast_to(top, (8, 128)), jnp.broadcast_to(mass, (8, 128))
    loss = jnp.log(mass) + top - pltpu.roll(top, 124, 1)
    loss = jnp.where(lane % 8 < 4, loss, pltpu.roll(loss, 4, 1))
    loss_ref[...] = spread(loss, lane, me)[0:1, :qcount]
    probs = shares / mass
    coef = (probs - pltpu.roll(probs, 124, 1)) / total
    coef = jnp.where(lane % 8 < 4, coef, pltpu.roll(coef, 4, 1))

    def make_scale(pair, carry):
        for which in range(2):
            wide = spread(coef, lane, peer_of(2 * pair + which))[0:pcount]
            scale[pair, :, which * block : (which + 1) * block] = (
                wide * rsum[pair, :, which * block : (which + 1) * block]
            )
        return carry

    lax.fori_loop(0, ROWS // 2, make_scale, 0)

    part[...] = jnp.zeros_like(part)

    def passage_grad(passage, carry):
        def pair_grad(pair, acc):
            weight = (expo[pair, passage] * scale[pair, pl.ds(passage, 1), :]).astype(BF16)
            start = pl.multiple_of(pair * 2 * block, 2 * block)
            return acc + jnp.dot(weight, qbuf[pl.ds(start, 2 * block), :], preferred_element_type=F32)

        d_embed = lax.fori_loop(0, ROWS // 2, pair_grad, jnp.zeros((ptok, width), F32))
        one = unit[passage]
        along = jnp.sum(d_embed * one, axis=1, keepdims=True)
        d_flat = ((d_embed - one * along) / norm[passage]).astype(BF16)
        grown = lax.dot_general(
            hidden_ref[passage], d_flat, (((0,), (0,)), ((), ())), preferred_element_type=F32
        )
        part[...] += grown.reshape(part.shape)
        return carry

    lax.fori_loop(0, pcount, passage_grad, 0)

    pair_copy = pltpu.make_async_remote_copy(
        src_ref=part.at[:, 1 - core], dst_ref=precv,
        send_sem=ps.at[0], recv_sem=ps.at[1], device_id=partner, device_id_type=MESH,
    )
    pair_copy.start()
    pair_copy.wait_recv()
    rsend[...] = part[:, core] + precv[...]

    def grad_copy(slot):
        return pltpu.make_async_remote_copy(
            src_ref=rsend.at[back_of(slot)], dst_ref=rrecv.at[slot],
            send_sem=rs.at[slot], recv_sem=rr.at[slot],
            device_id={"passage": back_of(slot)}, device_id_type=MESH,
        )

    for slot in range(1, ROWS):
        grad_copy(slot).start()
    acc = rsend[me]
    for slot in range(1, ROWS):
        grad_copy(slot).wait_recv()
        acc = acc + rrecv[slot]
    zbuf[mz] = acc

    def z_copy(step):
        return pltpu.make_async_remote_copy(
            src_ref=zbuf.at[mz], dst_ref=zbuf.at[mz],
            send_sem=zs.at[step], recv_sem=zr.at[step],
            device_id={"query": ((mz + step) % nz) * 2 + core}, device_id_type=MESH,
        )

    def z_arrival(step):
        source = (mz + nz - step) % nz
        return pltpu.make_async_remote_copy(
            src_ref=zbuf.at[source], dst_ref=zbuf.at[source],
            send_sem=zs.at[step], recv_sem=zr.at[step],
            device_id={"query": ((mz + step) % nz) * 2 + core}, device_id_type=MESH,
        )

    for step in range(1, nz):
        z_copy(step).start()
    for step in range(1, nz):
        z_arrival(step).wait_recv()
    acc = zbuf[0]
    for step in range(1, nz):
        acc = acc + zbuf[step]
    fin[core] = acc
    fin_copy = pltpu.make_async_remote_copy(
        src_ref=fin.at[core], dst_ref=fin.at[core],
        send_sem=fs.at[0], recv_sem=fs.at[1], device_id=partner, device_id_type=MESH,
    )
    fin_copy.start()
    for slot in range(1, ROWS):
        query_copy(slot).wait_send()
        meta_copy(slot).wait_send()
        score_copy(slot).wait_send()
        grad_copy(slot).wait_send()
    pair_copy.wait_send()
    for step in range(1, nz):
        z_copy(step).wait_send()
    fin_arrival = pltpu.make_async_remote_copy(
        src_ref=fin.at[1 - core], dst_ref=fin.at[1 - core],
        send_sem=fs.at[0], recv_sem=fs.at[1], device_id=partner, device_id_type=MESH,
    )
    fin_arrival.wait_recv()
    fin_copy.wait_send()
    grad_ref[...] = fin[...].reshape(grad_ref.shape)


def body(queries, hidden, proj, lists):
    qcount, qtok, width = queries.shape
    pcount, ptok, hwidth = hidden.shape
    nside = lax.axis_size("passage")
    nq = lax.axis_size("query")
    total = qcount * nq * nside
    share = hwidth // nside
    block = qcount * qtok
    pairs = nside // 2
    nz = nq // 2
    dma = pltpu.SemaphoreType.DMA
    losses, grad = pl.pallas_call(
        functools.partial(kernel, total),
        out_shape=(
            jax.ShapeDtypeStruct((1, qcount), F32),
            jax.ShapeDtypeStruct((share, width), F32),
        ),
        in_specs=[pl.BlockSpec(memory_space=pltpu.VMEM)] * 4,
        out_specs=(pl.BlockSpec(memory_space=pltpu.VMEM),) * 2,
        scratch_shapes=[
            pltpu.VMEM((nside * block, width), BF16),
            pltpu.VMEM((nside, 16, 128), BF16),
            pltpu.VMEM((128, 128), F32),
            pltpu.VMEM((128, 128), F32),
            pltpu.VMEM((pcount, ptok, width), BF16),
            pltpu.VMEM((pcount, ptok, width), F32),
            pltpu.VMEM((pcount, ptok, width), F32),
            pltpu.VMEM((pairs, pcount, ptok, 2 * block), F32),
            pltpu.VMEM((pairs, pcount, 2 * block), F32),
            pltpu.VMEM((nside, 8, 128), F32),
            pltpu.VMEM((pairs, pcount, 2 * block), F32),
            pltpu.VMEM((nside, 2, share // 2, width), F32),
            pltpu.VMEM((nside, share // 2, width), F32),
            pltpu.VMEM((nside, share // 2, width), F32),
            pltpu.VMEM((nside, share // 2, width), F32),
            pltpu.VMEM((nz, share // 2, width), F32),
            pltpu.VMEM((2, share // 2, width), F32),
            dma((nside,)), dma((nside,)),
            dma((nside,)), dma((nside,)),
            dma((nside,)), dma((nside,)),
            dma((2,)),
            dma((nside,)), dma((nside,)),
            dma((nz,)), dma((nz,)),
            dma((2,)),
        ],
        compiler_params=pltpu.CompilerParams(
            collective_id=0, has_side_effects=True, vmem_limit_bytes=60 * 1024 * 1024
        ),
        name="retriever_step",
    )(queries, hidden, proj, lists)
    return (losses.reshape(qcount), grad)


def solution(mesh):
    placed = (
        P(("query", "passage"), None, None),
        P(("query", "passage"), None, None),
        P(),
        P(("query", "passage"), None),
    )
    return jax.shard_map(
        body,
        mesh=mesh,
        in_specs=placed,
        out_specs=(P(("query", "passage")), P("passage", None)),
        check_vma=False,
    )
```

time: 562 us -> 72.2 us (0.13)
  waiting for transfers between devices: 484 us -> 0 us
  Pallas kernels: 0 us -> 66.4 us
  blocking collectives: 20 us -> 0 us
  matrix products: 14.4 us -> 0 us
  between operations: 14.2 us -> 0.64 us
  other arithmetic: 8.8 us -> 0 us
  starting transfers between devices: 8.45 us -> 0 us
  local copies, waits for them, and re-layouts: 10.5 us -> 4.88 us
    psum x1 -> x0, waiting for transfers between devices: 471 us -> none  [body(): full_grad = lax.psum(partial_grad, ('query', 'passage'))]
    pallas_call x0 -> x1, Pallas kernels: none -> 66.4 us  [body(): pl.pallas_call(functools.partial(kernel, total), out_shape=(jax.ShapeDtyp...]
    all_gather x1 -> x0, blocking collectives: 20 us -> none  [body(): gathered = lax.all_gather(queries, 'passage', axis=0, tiled=True)]
    dot_general x16 -> x0, matrix products: 14.4 us -> none  [the longest x4 4.46 us: grad_single(): lax.dot_general(emb, grad_qflat, (((1,), (1,)), ((), ())), preferred_elem...]
    all_to_all x2 -> x0, waiting for transfers between devices: 12.8 us -> none  [the longest x1 6.46 us: body(): lax.all_to_all(scores, 'passage', split_axis=0, concat_axis=1, tiled=True)]
    all_to_all x2 -> x0, starting transfers between devices: 8.41 us -> none  [the longest x1 4.93 us: body(): lax.all_to_all(scores, 'passage', split_axis=0, concat_axis=1, tiled=True)]
    reduce_sum x14 -> x0, other arithmetic: 7.24 us -> none  [the longest x4 3.96 us: grad_single(): probs = jax.nn.softmax(BETA * sims, axis=0)]
  transfers between devices with their start and end apart: 3 -> 0, of which waited for: 3 -> 0; matrix products, arithmetic and copies ran while one was open for 0% -> 0% of each run, Pallas kernels for 0% -> 0%
where the time goes in v1:
time: 72.2 us; the launch traced here: 72 us
  Pallas kernels  66.4 us (92%)
  local copies, waits for them, and re-layouts  4.88 us (7%)
    pallas_call x1, Pallas kernels, body(): pl.pallas_call(functools.partial(kernel, total), out_shape=(jax.ShapeDtyp...  66.4 us
    unnamed x3, local copies, waits for them, and re-layouts  4.88 us

profile of v1, /device:TPU:1, one launch (start us, length us, event | category | flops | bytes accessed | tf_op | source)
XLA Modules:
  0.0 72.0 jit_solution(2766922625637810848)
XLA Ops:
  0.6 2.4 %copy.6.hidden_ref = bf16[4,180,768]{2,1,0:T(8,128)(2,1)} copy(bf16[4,180,768]{2,0,1:T(4,128)(2,1)} %param.5) | data formatting | bytes 2211840 | tf_op args[1]
  3.0 66.4 %retriever_step.1 = (f32[1,4]{1,0:T(1,128)}, f32[48,128]{1,0:T(8,128)}) custom-call(bf16[4,32,128]{2,1,0:T(8,128)(2,1)} %queries_ref.1, bf16[4,180,768]{2,1,0:T(8,128)(2,1)} %copy.6.hidden_ref, bf16[768,128]{1,0:T(8,128)(2,1)} %proj_ref.1, s32[4,64]{1,0:T(4,128)} %lists_ref.1), custom_call_target="tpu_custom_call" | custom-call | tf_op jit(solution)/shard_map/retriever_step/pallas_call | solution.py:304
  69.4 1.2 %copy.9 = f32[4]{0:T(128)} copy(f32[4]{0:T(128)} %bitcast.1) | data formatting | bytes 32
  70.6 1.3 %copy.10 = f32[48,128]{1,0:T(8,128)} copy(f32[48,128]{1,0:T(8,128)} %get-tuple-element.9) | data formatting | bytes 49152

commit v2 on v1

--- a/solution.py
+++ b/solution.py
@@ -14,6 +14,7 @@
 F32 = jnp.float32
 BF16 = jnp.bfloat16
 NEGBIG = -3.0e38
+PARTS = 3
 MESH = pl.DeviceIdType.MESH
 
 
@@ -30,14 +31,15 @@
 
 def kernel(
     total,
+    queries_hbm, hidden_hbm, proj_hbm, lists_hbm,
+    loss_ref, grad_ref,
     queries_ref, hidden_ref, proj_ref, lists_ref,
-    loss_ref, grad_ref,
-    qbuf, meta, mrows, mcols, embed, unit, norm, expo, rsum, score, scale,
+    qbuf, meta, mrows, mcols, turned, embed, unit, norm, expo, rsum, score, scale,
     part, precv, rsend, rrecv, zbuf, fin,
-    qs, qr, ms, mr, ss, sr, ps, rs, rr, zs, zr, fs,
+    ins, qs, qr, ms, mr, ss, sr, ps, rs, rr, zs, zr, fs, tok,
 ):
     qcount, qtok, width = queries_ref.shape
-    pcount, ptok, hwidth = hidden_ref.shape
+    ptok, pcount, hwidth = hidden_ref.shape
     nz = lax.axis_size("query") // 2
     qid = lax.axis_index("query")
     me = lax.axis_index("passage")
@@ -46,6 +48,17 @@
     partner = {"query": mz * 2 + (1 - core)}
     block = qcount * qtok
     half = grad_ref.shape[0] // 2
+    piece = ptok * pcount // PARTS
+
+    def along(step):
+        return {"query": ((mz + nz + step) % nz) * 2 + core}
+
+    loads = [
+        pltpu.make_async_copy(src, dst, ins.at[n])
+        for n, (src, dst) in enumerate(
+            [(queries_hbm, queries_ref), (lists_hbm, lists_ref), (proj_hbm, proj_ref), (hidden_hbm, hidden_ref)]
+        )
+    ]
 
     def peer_of(slot):
         dx, dy = gray(slot // SIDE), gray(slot % SIDE)
@@ -59,14 +72,24 @@
     for slot in range(1, ROWS):
         pl.semaphore_signal(barrier, inc=1, device_id={"passage": peer_of(slot)}, device_id_type=MESH)
 
-    def greet(step, carry):
-        zpeer = (mz + step) % nz
-        pl.semaphore_signal(barrier, inc=1, device_id={"query": zpeer * 2 + core}, device_id_type=MESH)
-        return carry
-
-    lax.fori_loop(1, nz, greet, 0)
+    for step in (-1, 1):
+        pl.semaphore_signal(barrier, inc=1, device_id=along(step), device_id_type=MESH)
     pl.semaphore_signal(barrier, inc=1, device_id=partner, device_id_type=MESH)
-
+    for load in loads:
+        load.start()
+
+    def know_send(level):
+        for side, step in enumerate((1, -1)):
+            pl.semaphore_signal(
+                tok.at[level, side], inc=1, device_id=along(step * (1 << level)), device_id_type=MESH
+            )
+
+    def know_wait(level):
+        for side in range(2):
+            pl.semaphore_wait(tok.at[level, side], 1)
+
+    loads[0].wait()
+    loads[1].wait()
     lane = lax.broadcasted_iota(jnp.int32, (8, 128), 1)
     row = lax.broadcasted_iota(jnp.int32, (block, block), 0)
     col = lax.broadcasted_iota(jnp.int32, (block, block), 1)
@@ -89,7 +112,8 @@
     tile = jnp.concatenate(counts + firsts, axis=0)
     meta[0] = jnp.concatenate([tile, jnp.zeros_like(tile)], axis=0).astype(BF16)
 
-    pl.semaphore_wait(barrier, ROWS - 1 + nz - 1 + 1)
+    pl.semaphore_wait(barrier, ROWS - 1 + 2 + 1)
+    know_send(0)
 
     def query_copy(slot):
         return pltpu.make_async_remote_copy(
@@ -118,16 +142,24 @@
     for slot in range(1, ROWS):
         meta_copy(slot).start()
 
-    def project(passage, carry):
-        flat = jnp.dot(hidden_ref[passage], proj_ref[...], preferred_element_type=F32)
+    loads[2].wait()
+    loads[3].wait()
+
+    def project(chunk, carry):
+        rows = pl.ds(chunk * (ptok // PARTS), ptok // PARTS)
+        states = hidden_ref[rows].reshape(piece, hwidth)
+        turned[chunk] = states
+        flat = jnp.dot(states, proj_ref[...], preferred_element_type=F32)
         size = jnp.sqrt(jnp.sum(flat * flat, axis=1, keepdims=True) + EPS)
         one = flat / size
-        norm[passage] = jnp.broadcast_to(size, one.shape)
-        unit[passage] = one
-        embed[passage] = one.astype(BF16)
+        norm[chunk] = jnp.broadcast_to(size, one.shape)
+        unit[chunk] = one
+        embed[chunk] = one.astype(BF16)
         return carry
 
-    lax.fori_loop(0, pcount, project, 0)
+    lax.fori_loop(0, PARTS, project, 0)
+    know_wait(0)
+    know_send(1)
 
     def score_pair(pair, found):
         @pl.when(pair > 0)
@@ -137,18 +169,23 @@
         query_copy(2 * pair + 1).wait_recv()
         start = pl.multiple_of(pair * 2 * block, 2 * block)
         both = qbuf[pl.ds(start, 2 * block), :]
-        lses = []
-        for passage in range(pcount):
+        top = None
+        for chunk in range(PARTS):
             sims = lax.dot_general(
-                embed[passage], both, (((1,), (1,)), ((), ())), preferred_element_type=F32
+                embed[chunk], both, (((1,), (1,)), ((), ())), preferred_element_type=F32
             )
-            top = jnp.max(sims, axis=0, keepdims=True)
-            raised = jnp.exp(BETA * (sims - top))
-            expo[pair, passage] = raised
-            total_e = jnp.sum(raised, axis=0, keepdims=True)
-            rsum[pair, passage : passage + 1] = 1.0 / total_e
-            lses.append(jnp.log(total_e) + BETA * top)
-        lse = jnp.concatenate(lses + lses, axis=0)
+            expo[pair, chunk] = sims
+            most = jnp.max(sims.reshape(piece // 8, 8, 2 * block), axis=0)
+            top = most if top is None else jnp.maximum(top, most)
+        top = jnp.maximum(top, pltpu.roll(top, 4, 0))
+        mass = jnp.zeros_like(top)
+        for chunk in range(PARTS):
+            raised = jnp.exp(BETA * (expo[pair, chunk].reshape(piece // 8, 8, 2 * block) - top[None]))
+            expo[pair, chunk] = raised.reshape(piece, 2 * block)
+            mass = mass + jnp.sum(raised, axis=0)
+        mass = mass + pltpu.roll(mass, 4, 0)
+        rsum[pair] = 1.0 / mass
+        lse = jnp.log(mass) + BETA * top
         for which in range(2):
             summed = lse[:, which * block : (which + 1) * block]
             for step in (4, 8, 16, 32, 64):
@@ -162,6 +199,8 @@
     for slot in range(1, ROWS):
         score_copy(slot).start()
 
+    know_wait(1)
+    know_send(2)
     for slot in range(ROWS):
         if slot:
             meta_copy(slot).wait_recv()
@@ -191,10 +230,12 @@
     probs = shares / mass
     coef = (probs - pltpu.roll(probs, 124, 1)) / total
     coef = jnp.where(lane % 8 < 4, coef, pltpu.roll(coef, 4, 1))
+    sub = lax.broadcasted_iota(jnp.int32, (8, 128), 0)
+    coef = jnp.where(sub < 4, coef, pltpu.roll(coef, 4, 0))
 
     def make_scale(pair, carry):
         for which in range(2):
-            wide = spread(coef, lane, peer_of(2 * pair + which))[0:pcount]
+            wide = spread(coef, lane, peer_of(2 * pair + which))
             scale[pair, :, which * block : (which + 1) * block] = (
                 wide * rsum[pair, :, which * block : (which + 1) * block]
             )
@@ -202,25 +243,32 @@
 
     lax.fori_loop(0, ROWS // 2, make_scale, 0)
 
-    part[...] = jnp.zeros_like(part)
-
-    def passage_grad(passage, carry):
+    def chunk_grad(chunk, carry):
         def pair_grad(pair, acc):
-            weight = (expo[pair, passage] * scale[pair, pl.ds(passage, 1), :]).astype(BF16)
+            spreads = expo[pair, chunk].reshape(piece // 8, 8, 2 * block)
+            weight = (spreads * scale[pair][None]).reshape(piece, 2 * block).astype(BF16)
             start = pl.multiple_of(pair * 2 * block, 2 * block)
             return acc + jnp.dot(weight, qbuf[pl.ds(start, 2 * block), :], preferred_element_type=F32)
 
-        d_embed = lax.fori_loop(0, ROWS // 2, pair_grad, jnp.zeros((ptok, width), F32))
-        one = unit[passage]
-        along = jnp.sum(d_embed * one, axis=1, keepdims=True)
-        d_flat = ((d_embed - one * along) / norm[passage]).astype(BF16)
+        d_embed = lax.fori_loop(0, ROWS // 2, pair_grad, jnp.zeros((piece, width), F32))
+        one = unit[chunk]
+        inner = jnp.sum(d_embed * one, axis=1, keepdims=True)
+        d_flat = ((d_embed - one * inner) / norm[chunk]).astype(BF16)
         grown = lax.dot_general(
-            hidden_ref[passage], d_flat, (((0,), (0,)), ((), ())), preferred_element_type=F32
-        )
-        part[...] += grown.reshape(part.shape)
+            turned[chunk], d_flat, (((0,), (0,)), ((), ())), preferred_element_type=F32
+        ).reshape(part.shape)
+
+        @pl.when(chunk == 0)
+        def _():
+            part[...] = grown
+
+        @pl.when(chunk > 0)
+        def _():
+            part[...] += grown
+
         return carry
 
-    lax.fori_loop(0, pcount, passage_grad, 0)
+    lax.fori_loop(0, PARTS, chunk_grad, 0)
 
     pair_copy = pltpu.make_async_remote_copy(
         src_ref=part.at[:, 1 - core], dst_ref=precv,
@@ -260,6 +308,7 @@
             device_id={"query": ((mz + step) % nz) * 2 + core}, device_id_type=MESH,
         )
 
+    know_wait(2)
     for step in range(1, nz):
         z_copy(step).start()
     for step in range(1, nz):
@@ -297,6 +346,7 @@
     nq = lax.axis_size("query")
     total = qcount * nq * nside
     share = hwidth // nside
+    piece = ptok * pcount // PARTS
     block = qcount * qtok
     pairs = nside // 2
     nz = nq // 2
@@ -307,26 +357,32 @@
             jax.ShapeDtypeStruct((1, qcount), F32),
             jax.ShapeDtypeStruct((share, width), F32),
         ),
-        in_specs=[pl.BlockSpec(memory_space=pltpu.VMEM)] * 4,
+        in_specs=[pl.BlockSpec(memory_space=pl.ANY)] * 4,
         out_specs=(pl.BlockSpec(memory_space=pltpu.VMEM),) * 2,
         scratch_shapes=[
+            pltpu.VMEM(queries.shape, BF16),
+            pltpu.VMEM((ptok, pcount, hwidth), BF16),
+            pltpu.VMEM(proj.shape, BF16),
+            pltpu.VMEM(lists.shape, lists.dtype),
             pltpu.VMEM((nside * block, width), BF16),
             pltpu.VMEM((nside, 16, 128), BF16),
             pltpu.VMEM((128, 128), F32),
             pltpu.VMEM((128, 128), F32),
-            pltpu.VMEM((pcount, ptok, width), BF16),
-            pltpu.VMEM((pcount, ptok, width), F32),
-            pltpu.VMEM((pcount, ptok, width), F32),
-            pltpu.VMEM((pairs, pcount, ptok, 2 * block), F32),
-            pltpu.VMEM((pairs, pcount, 2 * block), F32),
+            pltpu.VMEM((PARTS, piece, hwidth), BF16),
+            pltpu.VMEM((PARTS, piece, width), BF16),
+            pltpu.VMEM((PARTS, piece, width), F32),
+            pltpu.VMEM((PARTS, piece, width), F32),
+            pltpu.VMEM((pairs, PARTS, piece, 2 * block), F32),
+            pltpu.VMEM((pairs, 8, 2 * block), F32),
             pltpu.VMEM((nside, 8, 128), F32),
-            pltpu.VMEM((pairs, pcount, 2 * block), F32),
+            pltpu.VMEM((pairs, 8, 2 * block), F32),
             pltpu.VMEM((nside, 2, share // 2, width), F32),
             pltpu.VMEM((nside, share // 2, width), F32),
             pltpu.VMEM((nside, share // 2, width), F32),
             pltpu.VMEM((nside, share // 2, width), F32),
             pltpu.VMEM((nz, share // 2, width), F32),
             pltpu.VMEM((2, share // 2, width), F32),
+            dma((4,)),
             dma((nside,)), dma((nside,)),
             dma((nside,)), dma((nside,)),
             dma((nside,)), dma((nside,)),
@@ -334,12 +390,13 @@
             dma((nside,)), dma((nside,)),
             dma((nz,)), dma((nz,)),
             dma((2,)),
+            pltpu.SemaphoreType.REGULAR((3, 2)),
         ],
         compiler_params=pltpu.CompilerParams(
             collective_id=0, has_side_effects=True, vmem_limit_bytes=60 * 1024 * 1024
         ),
         name="retriever_step",
-    )(queries, hidden, proj, lists)
+    )(queries, hidden.transpose(1, 0, 2), proj, lists)
     return (losses.reshape(qcount), grad)
 
 

time: 72.2 us -> 69.1 us (0.957)
  local copies, waits for them, and re-layouts: 4.88 us -> 2.52 us
    unnamed x3 -> x2, local copies, waits for them, and re-layouts: 4.88 us -> 2.52 us
where the time goes in v2:
time: 69.1 us; the launch traced here: 68.9 us
  Pallas kernels  65.7 us (95%)
  local copies, waits for them, and re-layouts  2.52 us (4%)
    pallas_call x1, Pallas kernels, body(): pl.pallas_call(functools.partial(kernel, total), out_shape=(jax.ShapeDtyp...  65.7 us
    unnamed x2, local copies, waits for them, and re-layouts  2.52 us

profile of v2, /device:TPU:1, one launch (start us, length us, event | category | flops | bytes accessed | tf_op | source)
XLA Modules:
  0.0 68.9 jit_solution(3171466675533739016)
XLA Ops:
  0.6 65.7 %retriever_step.1 = (f32[1,4]{1,0:T(1,128)}, f32[48,128]{1,0:T(8,128)}) custom-call(bf16[4,32,128]{2,1,0:T(8,128)(2,1)} %queries_hbm.1, bf16[180,4,768]{2,1,0:T(4,128)(2,1)} %bitcast.2, bf16[768,128]{1,0:T(8,128)(2,1)} %proj_hbm.1, s32[4,64]{1,0:T(4,128)} %lists_hbm.1), custom_call_target="tpu_custom_call" | custom-call | tf_op jit(solution)/shard_map/retriever_step/pallas_call | solution.py:354
  66.4 1.2 %copy.8 = f32[4]{0:T(128)} copy(f32[4]{0:T(128)} %bitcast.3) | data formatting | bytes 32
  67.6 1.3 %copy.9 = f32[48,128]{1,0:T(8,128)} copy(f32[48,128]{1,0:T(8,128)} %get-tuple-element.9) | data formatting | bytes 49152

commit v3 on v2

--- a/solution.py
+++ b/solution.py
@@ -1,4 +1,5 @@
 import functools
+import math
 
 import jax
 import jax.numpy as jnp
@@ -8,6 +9,7 @@
 from jax.sharding import PartitionSpec as P
 
 BETA = 4.0
+BETA2 = BETA * math.log2(math.e)
 EPS = 1e-06
 SIDE = 4
 ROWS = SIDE * SIDE
@@ -34,7 +36,7 @@
     queries_hbm, hidden_hbm, proj_hbm, lists_hbm,
     loss_ref, grad_ref,
     queries_ref, hidden_ref, proj_ref, lists_ref,
-    qbuf, meta, mrows, mcols, turned, embed, unit, norm, expo, rsum, score, scale,
+    qbuf, meta, mrows, mcols, turned, embed, unit, norm, expo, rsum, score, scale, d_flat,
     part, precv, rsend, rrecv, zbuf, fin,
     ins, qs, qr, ms, mr, ss, sr, ps, rs, rr, zs, zr, fs, tok,
 ):
@@ -148,7 +150,7 @@
     def project(chunk, carry):
         rows = pl.ds(chunk * (ptok // PARTS), ptok // PARTS)
         states = hidden_ref[rows].reshape(piece, hwidth)
-        turned[chunk] = states
+        turned[chunk] = states.T
         flat = jnp.dot(states, proj_ref[...], preferred_element_type=F32)
         size = jnp.sqrt(jnp.sum(flat * flat, axis=1, keepdims=True) + EPS)
         one = flat / size
@@ -180,7 +182,7 @@
         top = jnp.maximum(top, pltpu.roll(top, 4, 0))
         mass = jnp.zeros_like(top)
         for chunk in range(PARTS):
-            raised = jnp.exp(BETA * (expo[pair, chunk].reshape(piece // 8, 8, 2 * block) - top[None]))
+            raised = jnp.exp2(BETA2 * (expo[pair, chunk].reshape(piece // 8, 8, 2 * block) - top[None]))
             expo[pair, chunk] = raised.reshape(piece, 2 * block)
             mass = mass + jnp.sum(raised, axis=0)
         mass = mass + pltpu.roll(mass, 4, 0)
@@ -233,50 +235,43 @@
     sub = lax.broadcasted_iota(jnp.int32, (8, 128), 0)
     coef = jnp.where(sub < 4, coef, pltpu.roll(coef, 4, 0))
 
-    def make_scale(pair, carry):
+    for pair in range(ROWS // 2):
         for which in range(2):
             wide = spread(coef, lane, peer_of(2 * pair + which))
             scale[pair, :, which * block : (which + 1) * block] = (
                 wide * rsum[pair, :, which * block : (which + 1) * block]
             )
-        return carry
-
-    lax.fori_loop(0, ROWS // 2, make_scale, 0)
 
     def chunk_grad(chunk, carry):
-        def pair_grad(pair, acc):
+        d_embed = None
+        for pair in range(ROWS // 2):
             spreads = expo[pair, chunk].reshape(piece // 8, 8, 2 * block)
             weight = (spreads * scale[pair][None]).reshape(piece, 2 * block).astype(BF16)
-            start = pl.multiple_of(pair * 2 * block, 2 * block)
-            return acc + jnp.dot(weight, qbuf[pl.ds(start, 2 * block), :], preferred_element_type=F32)
-
-        d_embed = lax.fori_loop(0, ROWS // 2, pair_grad, jnp.zeros((piece, width), F32))
+            term = jnp.dot(
+                weight, qbuf[pair * 2 * block : (pair + 1) * 2 * block, :], preferred_element_type=F32
+            )
+            d_embed = term if d_embed is None else d_embed + term
         one = unit[chunk]
         inner = jnp.sum(d_embed * one, axis=1, keepdims=True)
-        d_flat = ((d_embed - one * inner) / norm[chunk]).astype(BF16)
-        grown = lax.dot_general(
-            turned[chunk], d_flat, (((0,), (0,)), ((), ())), preferred_element_type=F32
-        ).reshape(part.shape)
-
-        @pl.when(chunk == 0)
-        def _():
-            part[...] = grown
-
-        @pl.when(chunk > 0)
-        def _():
-            part[...] += grown
-
+        d_flat[chunk] = ((d_embed - one * inner) / norm[chunk]).astype(BF16)
         return carry
 
     lax.fori_loop(0, PARTS, chunk_grad, 0)
-
-    pair_copy = pltpu.make_async_remote_copy(
-        src_ref=part.at[:, 1 - core], dst_ref=precv,
-        send_sem=ps.at[0], recv_sem=ps.at[1], device_id=partner, device_id_type=MESH,
-    )
-    pair_copy.start()
-    pair_copy.wait_recv()
-    rsend[...] = part[:, core] + precv[...]
+    grown = None
+    for chunk in range(PARTS):
+        term = jnp.dot(turned[chunk], d_flat[chunk], preferred_element_type=F32)
+        grown = term if grown is None else grown + term
+    part[...] = grown.reshape(part.shape)
+
+    def pair_copy(ix):
+        line = pl.ds(((mx + SIDE - gray(ix)) % SIDE) * SIDE, SIDE)
+        return pltpu.make_async_remote_copy(
+            src_ref=part.at[line, 1 - core], dst_ref=precv.at[line],
+            send_sem=ps.at[0, ix], recv_sem=ps.at[1, ix], device_id=partner, device_id_type=MESH,
+        )
+
+    for ix in (3, 2, 1, 0):
+        pair_copy(ix).start()
 
     def grad_copy(slot):
         return pltpu.make_async_remote_copy(
@@ -285,8 +280,13 @@
             device_id={"passage": back_of(slot)}, device_id_type=MESH,
         )
 
-    for slot in range(1, ROWS):
-        grad_copy(slot).start()
+    for ix in (3, 2, 1, 0):
+        line = pl.ds(((mx + SIDE - gray(ix)) % SIDE) * SIDE, SIDE)
+        pair_copy(ix).wait_recv()
+        rsend[line] = part[line, core] + precv[line]
+        for iy in (3, 2, 1, 0):
+            if ix or iy:
+                grad_copy(ix * SIDE + iy).start()
     acc = rsend[me]
     for slot in range(1, ROWS):
         grad_copy(slot).wait_recv()
@@ -327,7 +327,8 @@
         meta_copy(slot).wait_send()
         score_copy(slot).wait_send()
         grad_copy(slot).wait_send()
-    pair_copy.wait_send()
+    for ix in range(SIDE):
+        pair_copy(ix).wait_send()
     for step in range(1, nz):
         z_copy(step).wait_send()
     fin_arrival = pltpu.make_async_remote_copy(
@@ -337,6 +338,11 @@
     fin_arrival.wait_recv()
     fin_copy.wait_send()
     grad_ref[...] = fin[...].reshape(grad_ref.shape)
+
+
+def hand_over(loss_in, grad_in, loss_ref, grad_ref):
+    loss_ref[...] = loss_in[...]
+    grad_ref[...] = grad_in[...]
 
 
 def body(queries, hidden, proj, lists):
@@ -368,7 +374,7 @@
             pltpu.VMEM((nside, 16, 128), BF16),
             pltpu.VMEM((128, 128), F32),
             pltpu.VMEM((128, 128), F32),
-            pltpu.VMEM((PARTS, piece, hwidth), BF16),
+            pltpu.VMEM((PARTS, hwidth, piece), BF16),
             pltpu.VMEM((PARTS, piece, width), BF16),
             pltpu.VMEM((PARTS, piece, width), F32),
             pltpu.VMEM((PARTS, piece, width), F32),
@@ -376,6 +382,7 @@
             pltpu.VMEM((pairs, 8, 2 * block), F32),
             pltpu.VMEM((nside, 8, 128), F32),
             pltpu.VMEM((pairs, 8, 2 * block), F32),
+            pltpu.VMEM((PARTS, piece, width), BF16),
             pltpu.VMEM((nside, 2, share // 2, width), F32),
             pltpu.VMEM((nside, share // 2, width), F32),
             pltpu.VMEM((nside, share // 2, width), F32),
@@ -386,7 +393,7 @@
             dma((nside,)), dma((nside,)),
             dma((nside,)), dma((nside,)),
             dma((nside,)), dma((nside,)),
-            dma((2,)),
+            dma((2, SIDE)),
             dma((nside,)), dma((nside,)),
             dma((nz,)), dma((nz,)),
             dma((2,)),
@@ -397,6 +404,16 @@
         ),
         name="retriever_step",
     )(queries, hidden.transpose(1, 0, 2), proj, lists)
+    losses, grad = pl.pallas_call(
+        hand_over,
+        out_shape=(
+            jax.ShapeDtypeStruct((1, qcount), F32),
+            jax.ShapeDtypeStruct((share, width), F32),
+        ),
+        in_specs=[pl.BlockSpec(memory_space=pltpu.VMEM)] * 2,
+        out_specs=(pl.BlockSpec(memory_space=pltpu.VMEM),) * 2,
+        name="outputs",
+    )(losses, grad)
     return (losses.reshape(qcount), grad)
 
 

time: 69.1 us -> 61.6 us (0.89)
  Pallas kernels: 65.7 us -> 60.8 us
  local copies, waits for them, and re-layouts: 2.52 us -> 0 us
    pallas_call x1, Pallas kernels: 65.7 us -> 59.4 us  [body(): pl.pallas_call(functools.partial(kernel, total), out_shape=(jax.ShapeDtyp...]
    unnamed x2 -> x0, local copies, waits for them, and re-layouts: 2.52 us -> none
    pallas_call x0 -> x1, Pallas kernels: none -> 1.36 us  [body(): pl.pallas_call(hand_over, out_shape=(jax.ShapeDtypeStruct((1, qcount), F3...]
where the time goes in v3:
time: 61.6 us; the launch traced here: 61.4 us
  Pallas kernels  60.8 us (99%)
  between operations  0.64 us (1%)
    pallas_call x1, Pallas kernels, body(): pl.pallas_call(functools.partial(kernel, total), out_shape=(jax.ShapeDtyp...  59.4 us
    pallas_call x1, Pallas kernels, body(): pl.pallas_call(hand_over, out_shape=(jax.ShapeDtypeStruct((1, qcount), F3...  1.36 us

profile of v3, /device:TPU:1, one launch (start us, length us, event | category | flops | bytes accessed | tf_op | source)
XLA Modules:
  0.0 61.4 jit_solution(1156263336473893170)
XLA Ops:
  0.6 59.4 %retriever_step.1 = (f32[1,4]{1,0:T(1,128)}, f32[48,128]{1,0:T(8,128)}) custom-call(bf16[4,32,128]{2,1,0:T(8,128)(2,1)} %queries_hbm.1, bf16[180,4,768]{2,1,0:T(4,128)(2,1)} %bitcast.2, bf16[768,128]{1,0:T(8,128)(2,1)} %proj_hbm.1, s32[4,64]{1,0:T(4,128)} %lists_hbm.1), custom_call_target="tpu_custom_call" | custom-call | tf_op jit(solution)/shard_map/retriever_step/pallas_call | solution.py:360
  60.0 1.4 %outputs.1 = (f32[1,4]{1,0:T(1,128)}, f32[48,128]{1,0:T(8,128)}) custom-call(f32[1,4]{1,0:T(1,128)} %get-tuple-element.6.loss_in, f32[48,128]{1,0:T(8,128)} %get-tuple-element.7.grad_in), custom_call_target="tpu_custom_call" | custom-call | tf_op jit(solution)/shard_map/outputs/pallas_call | solution.py:407

commit v4 on v3

--- a/solution.py
+++ b/solution.py
@@ -36,8 +36,8 @@
     queries_hbm, hidden_hbm, proj_hbm, lists_hbm,
     loss_ref, grad_ref,
     queries_ref, hidden_ref, proj_ref, lists_ref,
-    qbuf, meta, mrows, mcols, turned, embed, unit, norm, expo, rsum, score, scale, d_flat,
-    part, precv, rsend, rrecv, zbuf, fin,
+    qbuf, meta, mrows, mcols, turned, embed, unit, norm, expo, rsum, tops, score, scale, d_flat,
+    part, given, precv, own, rsend, rrecv, zbuf, fin,
     ins, qs, qr, ms, mr, ss, sr, ps, rs, rr, zs, zr, fs, tok,
 ):
     qcount, qtok, width = queries_ref.shape
@@ -112,7 +112,7 @@
         counts.append(jnp.sum(hit, axis=0, keepdims=True))
         firsts.append(hit[0:1, :])
     tile = jnp.concatenate(counts + firsts, axis=0)
-    meta[0] = jnp.concatenate([tile, jnp.zeros_like(tile)], axis=0).astype(BF16)
+    meta[0] = tile.astype(BF16)
 
     pl.semaphore_wait(barrier, ROWS - 1 + 2 + 1)
     know_send(0)
@@ -163,7 +163,7 @@
     know_wait(0)
     know_send(1)
 
-    def score_pair(pair, found):
+    def score_pair(pair, carry):
         @pl.when(pair > 0)
         def _():
             query_copy(2 * pair).wait_recv()
@@ -186,16 +186,19 @@
             expo[pair, chunk] = raised.reshape(piece, 2 * block)
             mass = mass + jnp.sum(raised, axis=0)
         mass = mass + pltpu.roll(mass, 4, 0)
-        rsum[pair] = 1.0 / mass
-        lse = jnp.log(mass) + BETA * top
+        rsum[pair] = mass
+        tops[pair] = top
+        return carry
+
+    lax.fori_loop(0, ROWS // 2, score_pair, 0)
+    found = jnp.zeros((8, 128), F32)
+    for pair in range(ROWS // 2):
+        lse = jnp.log(rsum[pair]) + BETA * tops[pair]
         for which in range(2):
             summed = lse[:, which * block : (which + 1) * block]
             for step in (4, 8, 16, 32, 64):
                 summed = summed + pltpu.roll(summed, step, 1)
             found = jnp.where(lane // 8 == peer_of(2 * pair + which), summed, found)
-        return found
-
-    found = lax.fori_loop(0, ROWS // 2, score_pair, jnp.zeros((8, 128), F32))
     score[0] = found / BETA
 
     for slot in range(1, ROWS):
@@ -206,7 +209,7 @@
     for slot in range(ROWS):
         if slot:
             meta_copy(slot).wait_recv()
-        mrows[pl.ds(pl.multiple_of(8 * peer_of(slot), 8), 8), :] = meta[slot].astype(F32)[0:8]
+        mrows[pl.ds(pl.multiple_of(8 * peer_of(slot), 8), 8), :] = meta[slot].astype(F32)
     mcols[...] = mrows[...].T
 
     top = jnp.full((8, 128), NEGBIG, F32)
@@ -239,7 +242,7 @@
         for which in range(2):
             wide = spread(coef, lane, peer_of(2 * pair + which))
             scale[pair, :, which * block : (which + 1) * block] = (
-                wide * rsum[pair, :, which * block : (which + 1) * block]
+                wide / rsum[pair, :, which * block : (which + 1) * block]
             )
 
     def chunk_grad(chunk, carry):
@@ -262,11 +265,12 @@
         term = jnp.dot(turned[chunk], d_flat[chunk], preferred_element_type=F32)
         grown = term if grown is None else grown + term
     part[...] = grown.reshape(part.shape)
+    given[...] = part[:, 1 - core].astype(BF16)
 
     def pair_copy(ix):
         line = pl.ds(((mx + SIDE - gray(ix)) % SIDE) * SIDE, SIDE)
         return pltpu.make_async_remote_copy(
-            src_ref=part.at[line, 1 - core], dst_ref=precv.at[line],
+            src_ref=given.at[line], dst_ref=precv.at[line],
             send_sem=ps.at[0, ix], recv_sem=ps.at[1, ix], device_id=partner, device_id_type=MESH,
         )
 
@@ -283,15 +287,16 @@
     for ix in (3, 2, 1, 0):
         line = pl.ds(((mx + SIDE - gray(ix)) % SIDE) * SIDE, SIDE)
         pair_copy(ix).wait_recv()
-        rsend[line] = part[line, core] + precv[line]
+        own[line] = part[line, core] + precv[line].astype(F32)
+        rsend[line] = own[line].astype(BF16)
         for iy in (3, 2, 1, 0):
             if ix or iy:
                 grad_copy(ix * SIDE + iy).start()
-    acc = rsend[me]
+    acc = own[me]
     for slot in range(1, ROWS):
         grad_copy(slot).wait_recv()
-        acc = acc + rrecv[slot]
-    zbuf[mz] = acc
+        acc = acc + rrecv[slot].astype(F32)
+    zbuf[mz] = acc.astype(BF16)
 
     def z_copy(step):
         return pltpu.make_async_remote_copy(
@@ -313,9 +318,9 @@
         z_copy(step).start()
     for step in range(1, nz):
         z_arrival(step).wait_recv()
-    acc = zbuf[0]
+    acc = zbuf[0].astype(F32)
     for step in range(1, nz):
-        acc = acc + zbuf[step]
+        acc = acc + zbuf[step].astype(F32)
     fin[core] = acc
     fin_copy = pltpu.make_async_remote_copy(
         src_ref=fin.at[core], dst_ref=fin.at[core],
@@ -371,7 +376,7 @@
             pltpu.VMEM(proj.shape, BF16),
             pltpu.VMEM(lists.shape, lists.dtype),
             pltpu.VMEM((nside * block, width), BF16),
-            pltpu.VMEM((nside, 16, 128), BF16),
+            pltpu.VMEM((nside, 8, 128), BF16),
             pltpu.VMEM((128, 128), F32),
             pltpu.VMEM((128, 128), F32),
             pltpu.VMEM((PARTS, hwidth, piece), BF16),
@@ -380,14 +385,17 @@
             pltpu.VMEM((PARTS, piece, width), F32),
             pltpu.VMEM((pairs, PARTS, piece, 2 * block), F32),
             pltpu.VMEM((pairs, 8, 2 * block), F32),
+            pltpu.VMEM((pairs, 8, 2 * block), F32),
             pltpu.VMEM((nside, 8, 128), F32),
             pltpu.VMEM((pairs, 8, 2 * block), F32),
             pltpu.VMEM((PARTS, piece, width), BF16),
             pltpu.VMEM((nside, 2, share // 2, width), F32),
+            pltpu.VMEM((nside, share // 2, width), BF16),
+            pltpu.VMEM((nside, share // 2, width), BF16),
             pltpu.VMEM((nside, share // 2, width), F32),
-            pltpu.VMEM((nside, share // 2, width), F32),
-            pltpu.VMEM((nside, share // 2, width), F32),
-            pltpu.VMEM((nz, share // 2, width), F32),
+            pltpu.VMEM((nside, share // 2, width), BF16),
+            pltpu.VMEM((nside, share // 2, width), BF16),
+            pltpu.VMEM((nz, share // 2, width), BF16),
             pltpu.VMEM((2, share // 2, width), F32),
             dma((4,)),
             dma((nside,)), dma((nside,)),

time: 61.6 us -> 53.7 us (0.87)
  Pallas kernels: 60.8 us -> 52.9 us
    pallas_call x1, Pallas kernels: 59.4 us -> 51.5 us  [body(): pl.pallas_call(functools.partial(kernel, total), out_shape=(jax.ShapeDtyp...]
where the time goes in v4:
time: 53.7 us; the launch traced here: 53.5 us
  Pallas kernels  52.9 us (99%)
  between operations  0.64 us (1%)
    pallas_call x1, Pallas kernels, body(): pl.pallas_call(functools.partial(kernel, total), out_shape=(jax.ShapeDtyp...  51.5 us
    pallas_call x1, Pallas kernels, body(): pl.pallas_call(hand_over, out_shape=(jax.ShapeDtypeStruct((1, qcount), F3...  1.36 us

profile of v4, /device:TPU:1, one launch (start us, length us, event | category | flops | bytes accessed | tf_op | source)
XLA Modules:
  0.0 53.5 jit_solution(6708879652812030798)
XLA Ops:
  0.6 51.5 %retriever_step.1 = (f32[1,4]{1,0:T(1,128)}, f32[48,128]{1,0:T(8,128)}) custom-call(bf16[4,32,128]{2,1,0:T(8,128)(2,1)} %queries_hbm.1, bf16[180,4,768]{2,1,0:T(4,128)(2,1)} %bitcast.2, bf16[768,128]{1,0:T(8,128)(2,1)} %proj_hbm.1, s32[4,64]{1,0:T(4,128)} %lists_hbm.1), custom_call_target="tpu_custom_call" | custom-call | tf_op jit(solution)/shard_map/retriever_step/pallas_call | solution.py:365
  52.2 1.4 %outputs.1 = (f32[1,4]{1,0:T(1,128)}, f32[48,128]{1,0:T(8,128)}) custom-call(f32[1,4]{1,0:T(1,128)} %get-tuple-element.6.loss_in, f32[48,128]{1,0:T(8,128)} %get-tuple-element.7.grad_in), custom_call_target="tpu_custom_call" | custom-call | tf_op jit(solution)/shard_map/outputs/pallas_call | solution.py:415

commit v5 on v4

--- a/solution.py
+++ b/solution.py
@@ -20,8 +20,38 @@
 MESH = pl.DeviceIdType.MESH
 
 
-def gray(index):
-    return index ^ (index >> 1)
+OFFSETS = (
+    (0, 0),
+    (1, 0), (-1, 0), (0, 1), (0, -1),
+    (1, 1), (-1, -1), (1, -1), (-1, 1), (2, 0), (0, 2),
+    (2, 1), (2, -1), (1, 2), (-1, 2),
+    (2, 2),
+)
+X1, X3, Y1, Y3 = (1, 0), (-1, 0), (0, 1), (0, -1)
+WAYS = {
+    (1, 0): (X1,), (-1, 0): (X3,), (0, 1): (Y1,), (0, -1): (Y3,),
+    (1, 1): (X1,), (-1, -1): (X3,), (1, -1): (Y3,), (-1, 1): (Y1,), (2, 0): (X1, X3), (0, 2): (Y1, Y3),
+    (2, 1): (X1, X3), (2, -1): (X1, X3), (1, 2): (Y1, Y3), (-1, 2): (Y1, Y3),
+    (2, 2): (X1, X3, Y1, Y3),
+}
+
+
+def wrapped(steps):
+    return (steps + 1) % SIDE - 1
+
+
+def make_hops():
+    hops = []
+    for offset in OFFSETS[1:]:
+        for share, via in enumerate(WAYS[offset]):
+            held = (wrapped(offset[0] - via[0]), wrapped(offset[1] - via[1]))
+            hops.append((OFFSETS.index(offset), via, OFFSETS.index(held), share, len(WAYS[offset])))
+    return tuple(hops)
+
+
+HOPS = make_hops()
+LINES = (2, -1, 1, 0)
+STAGES = ((4, 0, 2), (10, 2, 5), (14, 5, 7), (15, 7, 8))
 
 
 def spread(tile, lane, block):
@@ -62,18 +92,19 @@
         )
     ]
 
+    def at_offset(dx, dy):
+        return ((mx + SIDE + dx) % SIDE) * SIDE + (my + SIDE + dy) % SIDE
+
     def peer_of(slot):
-        dx, dy = gray(slot // SIDE), gray(slot % SIDE)
-        return ((mx + dx) % SIDE) * SIDE + (my + dy) % SIDE
+        return at_offset(*OFFSETS[slot])
 
     def back_of(slot):
-        dx, dy = gray(slot // SIDE), gray(slot % SIDE)
-        return ((mx + SIDE - dx) % SIDE) * SIDE + (my + SIDE - dy) % SIDE
+        dx, dy = OFFSETS[slot]
+        return at_offset(-dx, -dy)
 
     barrier = pltpu.get_barrier_semaphore()
-    for slot in range(1, ROWS):
-        pl.semaphore_signal(barrier, inc=1, device_id={"passage": peer_of(slot)}, device_id_type=MESH)
-
+    for dx, dy in (X1, X3, Y1, Y3):
+        pl.semaphore_signal(barrier, inc=1, device_id={"passage": at_offset(dx, dy)}, device_id_type=MESH)
     for step in (-1, 1):
         pl.semaphore_signal(barrier, inc=1, device_id=along(step), device_id_type=MESH)
     pl.semaphore_signal(barrier, inc=1, device_id=partner, device_id_type=MESH)
@@ -114,16 +145,28 @@
     tile = jnp.concatenate(counts + firsts, axis=0)
     meta[0] = tile.astype(BF16)
 
-    pl.semaphore_wait(barrier, ROWS - 1 + 2 + 1)
+    pl.semaphore_wait(barrier, 4 + 2 + 1)
     know_send(0)
 
-    def query_copy(slot):
-        return pltpu.make_async_remote_copy(
-            src_ref=qbuf.at[pl.ds(0, block)],
-            dst_ref=qbuf.at[pl.ds(slot * block, block)],
-            send_sem=qs.at[slot], recv_sem=qr.at[slot],
-            device_id={"passage": back_of(slot)}, device_id_type=MESH,
-        )
+    def query_hop(number):
+        slot, (dx, dy), held, share, shares = HOPS[number]
+        rows = block // shares
+        return pltpu.make_async_remote_copy(
+            src_ref=qbuf.at[pl.ds(held * block + share * rows, rows)],
+            dst_ref=qbuf.at[pl.ds(slot * block + share * rows, rows)],
+            send_sem=qs.at[number], recv_sem=qr.at[number],
+            device_id={"passage": at_offset(-dx, -dy)}, device_id_type=MESH,
+        )
+
+    def hand_on(slot):
+        for number, hop in enumerate(HOPS):
+            if hop[2] == slot:
+                query_hop(number).start()
+
+    def arrival(slot):
+        for number, hop in enumerate(HOPS):
+            if hop[0] == slot:
+                query_hop(number).wait_recv()
 
     def meta_copy(slot):
         return pltpu.make_async_remote_copy(
@@ -139,10 +182,7 @@
             device_id={"passage": back_of(slot)}, device_id_type=MESH,
         )
 
-    for slot in range(1, ROWS):
-        query_copy(slot).start()
-    for slot in range(1, ROWS):
-        meta_copy(slot).start()
+    hand_on(0)
 
     loads[2].wait()
     loads[3].wait()
@@ -164,11 +204,6 @@
     know_send(1)
 
     def score_pair(pair, carry):
-        @pl.when(pair > 0)
-        def _():
-            query_copy(2 * pair).wait_recv()
-
-        query_copy(2 * pair + 1).wait_recv()
         start = pl.multiple_of(pair * 2 * block, 2 * block)
         both = qbuf[pl.ds(start, 2 * block), :]
         top = None
@@ -190,7 +225,16 @@
         tops[pair] = top
         return carry
 
-    lax.fori_loop(0, ROWS // 2, score_pair, 0)
+    arrived = 0
+    for last, first_pair, end_pair in STAGES:
+        for slot in range(arrived + 1, last + 1):
+            arrival(slot)
+            hand_on(slot)
+        arrived = last
+        if last == ROWS - 1:
+            for slot in range(1, ROWS):
+                meta_copy(slot).start()
+        lax.fori_loop(first_pair, end_pair, score_pair, 0)
     found = jnp.zeros((8, 128), F32)
     for pair in range(ROWS // 2):
         lse = jnp.log(rsum[pair]) + BETA * tops[pair]
@@ -267,15 +311,16 @@
     part[...] = grown.reshape(part.shape)
     given[...] = part[:, 1 - core].astype(BF16)
 
-    def pair_copy(ix):
-        line = pl.ds(((mx + SIDE - gray(ix)) % SIDE) * SIDE, SIDE)
+    def pair_copy(dx):
+        line = pl.ds(((mx + SIDE - dx) % SIDE) * SIDE, SIDE)
+        ix = LINES.index(dx)
         return pltpu.make_async_remote_copy(
             src_ref=given.at[line], dst_ref=precv.at[line],
             send_sem=ps.at[0, ix], recv_sem=ps.at[1, ix], device_id=partner, device_id_type=MESH,
         )
 
-    for ix in (3, 2, 1, 0):
-        pair_copy(ix).start()
+    for dx in LINES:
+        pair_copy(dx).start()
 
     def grad_copy(slot):
         return pltpu.make_async_remote_copy(
@@ -284,14 +329,14 @@
             device_id={"passage": back_of(slot)}, device_id_type=MESH,
         )
 
-    for ix in (3, 2, 1, 0):
-        line = pl.ds(((mx + SIDE - gray(ix)) % SIDE) * SIDE, SIDE)
-        pair_copy(ix).wait_recv()
+    for dx in LINES:
+        line = pl.ds(((mx + SIDE - dx) % SIDE) * SIDE, SIDE)
+        pair_copy(dx).wait_recv()
         own[line] = part[line, core] + precv[line].astype(F32)
         rsend[line] = own[line].astype(BF16)
-        for iy in (3, 2, 1, 0):
-            if ix or iy:
-                grad_copy(ix * SIDE + iy).start()
+        for slot in range(ROWS - 1, 0, -1):
+            if OFFSETS[slot][0] == dx:
+                grad_copy(slot).start()
     acc = own[me]
     for slot in range(1, ROWS):
         grad_copy(slot).wait_recv()
@@ -327,13 +372,14 @@
         send_sem=fs.at[0], recv_sem=fs.at[1], device_id=partner, device_id_type=MESH,
     )
     fin_copy.start()
+    for number in range(len(HOPS)):
+        query_hop(number).wait_send()
     for slot in range(1, ROWS):
-        query_copy(slot).wait_send()
         meta_copy(slot).wait_send()
         score_copy(slot).wait_send()
         grad_copy(slot).wait_send()
-    for ix in range(SIDE):
-        pair_copy(ix).wait_send()
+    for dx in LINES:
+        pair_copy(dx).wait_send()
     for step in range(1, nz):
         z_copy(step).wait_send()
     fin_arrival = pltpu.make_async_remote_copy(
@@ -398,7 +444,7 @@
             pltpu.VMEM((nz, share // 2, width), BF16),
             pltpu.VMEM((2, share // 2, width), F32),
             dma((4,)),
-            dma((nside,)), dma((nside,)),
+            dma((len(HOPS),)), dma((len(HOPS),)),
             dma((nside,)), dma((nside,)),
             dma((nside,)), dma((nside,)),
             dma((2, SIDE)),

time: 53.7 us -> 57.1 us (1.063)
  Pallas kernels: 52.9 us -> 56.2 us
    pallas_call x1, Pallas kernels: 51.5 us -> 54.9 us  [body(): pl.pallas_call(functools.partial(kernel, total), out_shape=(jax.ShapeDtyp...]
where the time goes in v5:
time: 57.1 us; the launch traced here: 56.9 us
  Pallas kernels  56.2 us (98%)
  between operations  0.64 us (1%)
    pallas_call x1, Pallas kernels, body(): pl.pallas_call(functools.partial(kernel, total), out_shape=(jax.ShapeDtyp...  54.9 us
    pallas_call x1, Pallas kernels, body(): pl.pallas_call(hand_over, out_shape=(jax.ShapeDtypeStruct((1, qcount), F3...  1.36 us

profile of v5, /device:TPU:1, one launch (start us, length us, event | category | flops | bytes accessed | tf_op | source)
XLA Modules:
  0.0 56.9 jit_solution(2022513804348033341)
XLA Ops:
  0.6 54.9 %retriever_step.1 = (f32[1,4]{1,0:T(1,128)}, f32[48,128]{1,0:T(8,128)}) custom-call(bf16[4,32,128]{2,1,0:T(8,128)(2,1)} %queries_hbm.1, bf16[180,4,768]{2,1,0:T(4,128)(2,1)} %bitcast.2, bf16[768,128]{1,0:T(8,128)(2,1)} %proj_hbm.1, s32[4,64]{1,0:T(4,128)} %lists_hbm.1), custom_call_target="tpu_custom_call" | custom-call | tf_op jit(solution)/shard_map/retriever_step/pallas_call | solution.py:411
  55.5 1.4 %outputs.1 = (f32[1,4]{1,0:T(1,128)}, f32[48,128]{1,0:T(8,128)}) custom-call(f32[1,4]{1,0:T(1,128)} %get-tuple-element.6.loss_in, f32[48,128]{1,0:T(8,128)} %get-tuple-element.7.grad_in), custom_call_target="tpu_custom_call" | custom-call | tf_op jit(solution)/shard_map/outputs/pallas_call | solution.py:461

commit v6 on v4

--- a/solution.py
+++ b/solution.py
@@ -163,34 +163,39 @@
     know_wait(0)
     know_send(1)
 
-    def score_pair(pair, carry):
-        @pl.when(pair > 0)
+    def score_quad(quad, carry):
+        @pl.when(quad > 0)
         def _():
-            query_copy(2 * pair).wait_recv()
-
-        query_copy(2 * pair + 1).wait_recv()
-        start = pl.multiple_of(pair * 2 * block, 2 * block)
-        both = qbuf[pl.ds(start, 2 * block), :]
-        top = None
-        for chunk in range(PARTS):
-            sims = lax.dot_general(
-                embed[chunk], both, (((1,), (1,)), ((), ())), preferred_element_type=F32
-            )
-            expo[pair, chunk] = sims
-            most = jnp.max(sims.reshape(piece // 8, 8, 2 * block), axis=0)
-            top = most if top is None else jnp.maximum(top, most)
-        top = jnp.maximum(top, pltpu.roll(top, 4, 0))
-        mass = jnp.zeros_like(top)
-        for chunk in range(PARTS):
-            raised = jnp.exp2(BETA2 * (expo[pair, chunk].reshape(piece // 8, 8, 2 * block) - top[None]))
-            expo[pair, chunk] = raised.reshape(piece, 2 * block)
-            mass = mass + jnp.sum(raised, axis=0)
-        mass = mass + pltpu.roll(mass, 4, 0)
-        rsum[pair] = mass
-        tops[pair] = top
+            query_copy(4 * quad).wait_recv()
+
+        for which in range(1, 4):
+            query_copy(4 * quad + which).wait_recv()
+        raw = []
+        for which in range(2):
+            start = pl.multiple_of((2 * quad + which) * 2 * block, 2 * block)
+            both = qbuf[pl.ds(start, 2 * block), :]
+            top, kept = None, []
+            for chunk in range(PARTS):
+                sims = lax.dot_general(
+                    embed[chunk], both, (((1,), (1,)), ((), ())), preferred_element_type=F32
+                ).reshape(piece // 8, 8, 2 * block)
+                kept.append(sims)
+                most = jnp.max(sims, axis=0)
+                top = most if top is None else jnp.maximum(top, most)
+            raw.append((kept, jnp.maximum(top, pltpu.roll(top, 4, 0))))
+        for which in range(2):
+            pair = 2 * quad + which
+            kept, top = raw[which]
+            mass = jnp.zeros_like(top)
+            for chunk in range(PARTS):
+                raised = jnp.exp2(BETA2 * (kept[chunk] - top[None]))
+                expo[pair, chunk] = raised.reshape(piece, 2 * block)
+                mass = mass + jnp.sum(raised, axis=0)
+            rsum[pair] = mass + pltpu.roll(mass, 4, 0)
+            tops[pair] = top
         return carry
 
-    lax.fori_loop(0, ROWS // 2, score_pair, 0)
+    lax.fori_loop(0, ROWS // 4, score_quad, 0)
     found = jnp.zeros((8, 128), F32)
     for pair in range(ROWS // 2):
         lse = jnp.log(rsum[pair]) + BETA * tops[pair]
@@ -314,7 +319,7 @@
         )
 
     know_wait(2)
-    for step in range(1, nz):
+    for step in (8, 7, 9, 6, 10, 5, 11, 4, 12, 3, 13, 2, 14, 1, 15):
         z_copy(step).start()
     for step in range(1, nz):
         z_arrival(step).wait_recv()

time: 53.7 us -> 50.1 us (0.933)
  Pallas kernels: 52.9 us -> 49.3 us
    pallas_call x1, Pallas kernels: 51.5 us -> 47.9 us  [body(): pl.pallas_call(functools.partial(kernel, total), out_shape=(jax.ShapeDtyp...]
where the time goes in v6:
time: 50.1 us; the launch traced here: 49.9 us
  Pallas kernels  49.3 us (98%)
  between operations  0.64 us (1%)
    pallas_call x1, Pallas kernels, body(): pl.pallas_call(functools.partial(kernel, total), out_shape=(jax.ShapeDtyp...  47.9 us
    pallas_call x1, Pallas kernels, body(): pl.pallas_call(hand_over, out_shape=(jax.ShapeDtypeStruct((1, qcount), F3...  1.36 us

profile of v6, /device:TPU:1, one launch (start us, length us, event | category | flops | bytes accessed | tf_op | source)
XLA Modules:
  0.0 49.9 jit_solution(16958512297376258691)
XLA Ops:
  0.6 47.9 %retriever_step.1 = (f32[1,4]{1,0:T(1,128)}, f32[48,128]{1,0:T(8,128)}) custom-call(bf16[4,32,128]{2,1,0:T(8,128)(2,1)} %queries_hbm.1, bf16[180,4,768]{2,1,0:T(4,128)(2,1)} %bitcast.2, bf16[768,128]{1,0:T(8,128)(2,1)} %proj_hbm.1, s32[4,64]{1,0:T(4,128)} %lists_hbm.1), custom_call_target="tpu_custom_call" | custom-call | tf_op jit(solution)/shard_map/retriever_step/pallas_call | solution.py:370
  48.6 1.4 %outputs.1 = (f32[1,4]{1,0:T(1,128)}, f32[48,128]{1,0:T(8,128)}) custom-call(f32[1,4]{1,0:T(1,128)} %get-tuple-element.6.loss_in, f32[48,128]{1,0:T(8,128)} %get-tuple-element.7.grad_in), custom_call_target="tpu_custom_call" | custom-call | tf_op jit(solution)/shard_map/outputs/pallas_call | solution.py:420

commit v7 on v6

--- a/solution.py
+++ b/solution.py
@@ -141,8 +141,6 @@
 
     for slot in range(1, ROWS):
         query_copy(slot).start()
-    for slot in range(1, ROWS):
-        meta_copy(slot).start()
 
     loads[2].wait()
     loads[3].wait()
@@ -196,6 +194,8 @@
         return carry
 
     lax.fori_loop(0, ROWS // 4, score_quad, 0)
+    for slot in range(1, ROWS):
+        meta_copy(slot).start()
     found = jnp.zeros((8, 128), F32)
     for pair in range(ROWS // 2):
         lse = jnp.log(rsum[pair]) + BETA * tops[pair]
@@ -370,8 +370,8 @@
     losses, grad = pl.pallas_call(
         functools.partial(kernel, total),
         out_shape=(
-            jax.ShapeDtypeStruct((1, qcount), F32),
-            jax.ShapeDtypeStruct((share, width), F32),
+            pltpu.VMEM((1, qcount), F32),
+            pltpu.VMEM((share, width), F32),
         ),
         in_specs=[pl.BlockSpec(memory_space=pl.ANY)] * 4,
         out_specs=(pl.BlockSpec(memory_space=pltpu.VMEM),) * 2,
@@ -426,7 +426,10 @@
         in_specs=[pl.BlockSpec(memory_space=pltpu.VMEM)] * 2,
         out_specs=(pl.BlockSpec(memory_space=pltpu.VMEM),) * 2,
         name="outputs",
-    )(losses, grad)
+    )(
+        pltpu.with_memory_space_constraint(losses, pltpu.VMEM),
+        pltpu.with_memory_space_constraint(grad, pltpu.VMEM),
+    )
     return (losses.reshape(qcount), grad)
 
 

time: 50.1 us -> 48.9 us (0.976)
  Pallas kernels: 49.3 us -> 48.1 us
    pallas_call x1, Pallas kernels: 1.36 us -> 0.62 us  [body(): pl.pallas_call(hand_over, out_shape=(jax.ShapeDtypeStruct((1, qcount), F3...]
where the time goes in v7:
time: 48.9 us; the launch traced here: 48.7 us
  Pallas kernels  48.1 us (98%)
  between operations  0.64 us (1%)
    pallas_call x1, Pallas kernels, body(): pl.pallas_call(functools.partial(kernel, total), out_shape=(pltpu.VMEM((1...  47.5 us

profile of v7, /device:TPU:1, one launch (start us, length us, event | category | flops | bytes accessed | tf_op | source)
XLA Modules:
  0.0 48.7 jit_solution(1580468549320136696)
XLA Ops:
  0.6 47.5 %retriever_step.1 = (f32[1,4]{1,0:T(1,128)S(1)}, f32[48,128]{1,0:T(8,128)S(1)}) custom-call(bf16[4,32,128]{2,1,0:T(8,128)(2,1)} %queries_hbm.1, bf16[180,4,768]{2,1,0:T(4,128)(2,1)} %bitcast.2, bf16[768,128]{1,0:T(8,128)(2,1)} %proj_hbm.1, s32[4,64]{1,0:T(4,128)} %lists_hbm.1), custom_call_target="tpu_custom_call" | custom-call | tf_op jit(solution)/shard_map/retriever_step/pallas_call | solution.py:370
  48.1 0.6 %outputs.1 = (f32[1,4]{1,0:T(1,128)}, f32[48,128]{1,0:T(8,128)}) custom-call(f32[1,4]{1,0:T(1,128)S(1)} %get-tuple-element.6.loss_in, f32[48,128]{1,0:T(8,128)S(1)} %get-tuple-element.7.grad_in), custom_call_target="tpu_custom_call" | custom-call | tf_op jit(solution)/shard_map/outputs/pallas_call | solution.py:420

commit v8 on v7

--- a/solution.py
+++ b/solution.py
@@ -264,7 +264,8 @@
         d_flat[chunk] = ((d_embed - one * inner) / norm[chunk]).astype(BF16)
         return carry
 
-    lax.fori_loop(0, PARTS, chunk_grad, 0)
+    for chunk in range(PARTS):
+        chunk_grad(chunk, 0)
     grown = None
     for chunk in range(PARTS):
         term = jnp.dot(turned[chunk], d_flat[chunk], preferred_element_type=F32)

time: 48.9 us -> 48.1 us (0.984)
  Pallas kernels: 48.1 us -> 47.3 us
    pallas_call x1, Pallas kernels: 47.5 us -> 46.7 us  [body(): pl.pallas_call(functools.partial(kernel, total), out_shape=(pltpu.VMEM((1...]
where the time goes in v8:
time: 48.1 us; the launch traced here: 48 us
  Pallas kernels  47.3 us (98%)
  between operations  0.64 us (1%)
    pallas_call x1, Pallas kernels, body(): pl.pallas_call(functools.partial(kernel, total), out_shape=(pltpu.VMEM((1...  46.7 us

profile of v8, /device:TPU:1, one launch (start us, length us, event | category | flops | bytes accessed | tf_op | source)
XLA Modules:
  0.0 48.0 jit_solution(7607875427481419727)
XLA Ops:
  0.6 46.7 %retriever_step.1 = (f32[1,4]{1,0:T(1,128)S(1)}, f32[48,128]{1,0:T(8,128)S(1)}) custom-call(bf16[4,32,128]{2,1,0:T(8,128)(2,1)} %queries_hbm.1, bf16[180,4,768]{2,1,0:T(4,128)(2,1)} %bitcast.2, bf16[768,128]{1,0:T(8,128)(2,1)} %proj_hbm.1, s32[4,64]{1,0:T(4,128)} %lists_hbm.1), custom_call_target="tpu_custom_call" | custom-call | tf_op jit(solution)/shard_map/retriever_step/pallas_call | solution.py:371
  47.4 0.6 %outputs.1 = (f32[1,4]{1,0:T(1,128)}, f32[48,128]{1,0:T(8,128)}) custom-call(f32[1,4]{1,0:T(1,128)S(1)} %get-tuple-element.6.loss_in, f32[48,128]{1,0:T(8,128)S(1)} %get-tuple-element.7.grad_in), custom_call_target="tpu_custom_call" | custom-call | tf_op jit(solution)/shard_map/outputs/pallas_call | solution.py:421

commit v9 on v8

--- a/solution.py
+++ b/solution.py
@@ -152,7 +152,7 @@
         flat = jnp.dot(states, proj_ref[...], preferred_element_type=F32)
         size = jnp.sqrt(jnp.sum(flat * flat, axis=1, keepdims=True) + EPS)
         one = flat / size
-        norm[chunk] = jnp.broadcast_to(size, one.shape)
+        norm[chunk] = jnp.broadcast_to(1.0 / size, one.shape)
         unit[chunk] = one
         embed[chunk] = one.astype(BF16)
         return carry
@@ -261,7 +261,7 @@
             d_embed = term if d_embed is None else d_embed + term
         one = unit[chunk]
         inner = jnp.sum(d_embed * one, axis=1, keepdims=True)
-        d_flat[chunk] = ((d_embed - one * inner) / norm[chunk]).astype(BF16)
+        d_flat[chunk] = ((d_embed - one * inner) * norm[chunk]).astype(BF16)
         return carry
 
     for chunk in range(PARTS):

time: 48.1 us -> 48.1 us (level)
  no operation moved by 1% of the time
where the time goes in v9:
time: 48.1 us; the launch traced here: 48 us
  Pallas kernels  47.3 us (98%)
  between operations  0.64 us (1%)
    pallas_call x1, Pallas kernels, body(): pl.pallas_call(functools.partial(kernel, total), out_shape=(pltpu.VMEM((1...  46.7 us

profile of v9, /device:TPU:1, one launch (start us, length us, event | category | flops | bytes accessed | tf_op | source)
XLA Modules:
  0.0 48.0 jit_solution(14640616321607406424)
XLA Ops:
  0.6 46.7 %retriever_step.1 = (f32[1,4]{1,0:T(1,128)S(1)}, f32[48,128]{1,0:T(8,128)S(1)}) custom-call(bf16[4,32,128]{2,1,0:T(8,128)(2,1)} %queries_hbm.1, bf16[180,4,768]{2,1,0:T(4,128)(2,1)} %bitcast.2, bf16[768,128]{1,0:T(8,128)(2,1)} %proj_hbm.1, s32[4,64]{1,0:T(4,128)} %lists_hbm.1), custom_call_target="tpu_custom_call" | custom-call | tf_op jit(solution)/shard_map/retriever_step/pallas_call | solution.py:371
  47.4 0.6 %outputs.1 = (f32[1,4]{1,0:T(1,128)}, f32[48,128]{1,0:T(8,128)}) custom-call(f32[1,4]{1,0:T(1,128)S(1)} %get-tuple-element.6.loss_in, f32[48,128]{1,0:T(8,128)S(1)} %get-tuple-element.7.grad_in), custom_call_target="tpu_custom_call" | custom-call | tf_op jit(solution)/shard_map/outputs/pallas_call | solution.py:421
